TPU v7x, 256 devices: a whole 4x4x8 slice. The times are simulated.
256 devices in a mesh: pts: 8 (over z_lo, core), coord: 32 (over y, z_hi, x).
Axes of the slice: x: 4, y: 4, z: 8 (z_hi: 2, z_lo: 4; z = z_hi * 4 + z_lo), core: 2. Of those that a mesh axis runs over, the one named last changes fastest.
Arguments:
- point_seed: int32 [512], P('pts'), may hold values from 0 to 16777215
- pert_seed: int32 [512, 16], P('pts'), may hold values from 0 to 16777215
- source_coef: float32 [100000], P('coord'), may hold values from -9 to 9
- w1: bfloat16 [1024, 100000], P(None, 'coord'), may hold values from -0.009765625 to 0.009765625
- b1: float32 [1024], replicated, may hold values from -3 to 3
- w2: bfloat16 [1024, 1024], replicated, may hold values from -0.1875 to 0.1875
- w3: bfloat16 [1024], replicated, may hold values from -0.1875 to 0.1875
Outputs:
- residual: float32 [512], P(('pts', 'coord'))
- grad_w1: bfloat16 [1024, 100000], P('pts', 'coord')
- grad_w2: float32 [1024, 1024], P('coord')
- grad_b1: float32 [1024], P('coord')
- grad_w3: float32 [1024], P('coord')
All inputs are finite; a program needn't handle non-finite values.
Results may differ from a plain program's by a relative error of at most 0.023.
Values may be sent and summed in bfloat16 or wider, within the bound.
A program may use at most 128 MiB of HBM per device.

v0:
```python
import math
import jax
import jax.numpy as jnp
from jax import lax
from jax.sharding import PartitionSpec as P

D = 100000
hash_factor = 73244475
NOISE_SCALE = 2.0
READOUT = 0.0625


def shuffle_bits(packed_bits):
    return packed_bits ^ lax.shift_right_logical(packed_bits, jnp.full_like(packed_bits, 16))


def mix_bits(packed_bits):
    packed_bits = shuffle_bits(packed_bits)
    packed_bits = shuffle_bits(packed_bits * hash_factor)
    return shuffle_bits(packed_bits * hash_factor)


def to_unit(packed_bits):
    return ((packed_bits & 8388607).astype(jnp.float32) + 0.5) * (1.0 / 8388608.0)


def column_keys(columns):
    return (mix_bits(columns * 4), mix_bits(columns * 4 + 1), mix_bits(columns * 4 + 2))


def perturbed_rows(point_seeds, pert_seeds, column_hash, coef_part):
    key_zero, key_one, key_two = column_hash
    count_points, count_samples = pert_seeds.shape
    uniform_point = to_unit(mix_bits(key_two[None, :] ^ point_seeds[:, None]))
    coords = 2.0 * uniform_point - 1.0
    uniform_zero = to_unit(mix_bits(key_zero[None, None, :] ^ pert_seeds[:, :, None]))
    uniform_one = to_unit(mix_bits(key_one[None, None, :] ^ pert_seeds[:, :, None]))
    noise_draw = jnp.sqrt(-2.0 * jnp.log(uniform_zero)) * jnp.cos(2.0 * jnp.pi * uniform_one)
    shifted = (coords[:, None, :] + NOISE_SCALE * noise_draw).astype(jnp.bfloat16)
    shifted = shifted.reshape(count_points * count_samples, coords.shape[1])
    squares = jnp.sum(noise_draw * noise_draw, axis=2).reshape(count_points * count_samples)
    source = jnp.sum(coef_part[None, :] * jnp.sin(jnp.pi * coords), axis=1) / math.sqrt(D)
    return (shifted, squares, source)


def hidden_pass(pre_first, squares, source, w2, w3, count_samples):
    hidden_one = jnp.tanh(pre_first).astype(jnp.bfloat16)
    pre_second = lax.dot_general(
        hidden_one, w2, (((1,), (1,)), ((), ())), preferred_element_type=jnp.float32
    )
    hidden_two = jnp.tanh(pre_second).astype(jnp.bfloat16)
    values_out = READOUT * jnp.dot(hidden_two, w3, preferred_element_type=jnp.float32)
    stein_weight = (squares - D) / (NOISE_SCALE * NOISE_SCALE * count_samples)
    per_point = (stein_weight * values_out).reshape(-1, count_samples)
    residual = jnp.sum(per_point, axis=1) - source
    grad_values = (residual[:, None] * stein_weight.reshape(-1, count_samples)).reshape(-1)
    two_float = hidden_two.astype(jnp.float32)
    grad_readout = READOUT * jnp.sum(grad_values[:, None] * two_float, axis=0)
    grad_pre_two = (
        READOUT
        * grad_values[:, None]
        * w3.astype(jnp.float32)[None, :]
        * (1.0 - two_float * two_float)
    ).astype(jnp.bfloat16)
    grad_second = lax.dot_general(
        grad_pre_two, hidden_one, (((0,), (0,)), ((), ())), preferred_element_type=jnp.float32
    )
    grad_hidden = jnp.dot(grad_pre_two, w2, preferred_element_type=jnp.float32)
    one_float = hidden_one.astype(jnp.float32)
    grad_pre_one = (grad_hidden * (1.0 - one_float * one_float)).astype(jnp.bfloat16)
    grad_bias = jnp.sum(grad_pre_one.astype(jnp.float32), axis=0)
    return (residual, grad_pre_one, grad_second, grad_bias, grad_readout, hidden_one, grad_pre_two)


def shards(point_seed, pert_seed, source_coef, w1, b1, w2, w3):
    coord_count = lax.axis_size("coord")
    coord_width = w1.shape[1]
    points_here, samples = pert_seed.shape
    rows_here = points_here * samples
    rows_local = rows_here // coord_count
    points_local = points_here // coord_count
    coord_index = lax.axis_index("coord")
    columns = coord_index * coord_width + jnp.arange(coord_width, dtype=jnp.int32)
    column_hash = column_keys(columns)
    shifted, squares, source = perturbed_rows(point_seed, pert_seed, column_hash, source_coef)
    picked = shifted
    pre_local = lax.psum_scatter(
        lax.dot_general(picked, w1, (((1,), (1,)), ((), ())), preferred_element_type=jnp.float32),
        "coord",
        scatter_dimension=0,
        tiled=True,
    )
    squares_all, source_all = lax.psum((squares, source), "coord")
    squares_local = lax.dynamic_slice_in_dim(squares_all, coord_index * rows_local, rows_local, 0)
    source_local = lax.dynamic_slice_in_dim(source_all, coord_index * points_local, points_local, 0)
    residual, grad_pre_one, grad_second, grad_bias, grad_readout, hidden_one, grad_pre_two = (
        hidden_pass(pre_local + b1[None, :], squares_local, source_local, w2, w3, samples)
    )
    grad_rows = lax.all_gather(grad_pre_one, "coord", axis=0, tiled=True)
    picked = grad_rows
    grad_first = lax.psum_scatter(
        lax.dot_general(
            picked, shifted, (((0,), (0,)), ((), ())), preferred_element_type=jnp.float32
        ).astype(jnp.bfloat16),
        "pts",
        scatter_dimension=0,
        tiled=True,
    )
    share_second, share_bias, share_readout = (
        lax.psum_scatter(
            grad_second.astype(jnp.bfloat16), "coord", scatter_dimension=0, tiled=True
        ).astype(jnp.float32),
        lax.psum_scatter(
            grad_bias.astype(jnp.bfloat16), "coord", scatter_dimension=0, tiled=True
        ).astype(jnp.float32),
        lax.psum_scatter(
            grad_readout.astype(jnp.bfloat16), "coord", scatter_dimension=0, tiled=True
        ).astype(jnp.float32),
    )
    out_second, out_bias, out_readout = (
        lax.psum(share_second.astype(jnp.bfloat16), "pts").astype(jnp.float32),
        lax.psum(share_bias.astype(jnp.bfloat16), "pts").astype(jnp.float32),
        lax.psum(share_readout.astype(jnp.bfloat16), "pts").astype(jnp.float32),
    )
    return (residual, grad_first, out_second, out_bias, out_readout)


def solution(mesh):
    return jax.shard_map(
        shards,
        mesh=mesh,
        in_specs=(P("pts"), P("pts", None), P("coord"), P(None, "coord"), P(), P(), P()),
        out_specs=(
            P(("pts", "coord")),
            P("pts", "coord"),
            P("coord", None),
            P("coord"),
            P("coord"),
        ),
        check_vma=False,
    )
```

profile of v0, /device:TPU:1, one launch (start us, length us, event | category | flops | bytes accessed | tf_op | source)
XLA Modules:
  0.0 800.5 jit_solution(16428335105259536183)
XLA Ops:
  7.2 0.0 copy-start
  7.2 0.0 reduce-scatter.6.cloned.1.call-start
  7.3 0.9 copy.17
  8.2 0.1 xor.202
  8.3 0.0 slice-start
  8.3 4.2 multiply_reduce_fusion
  12.4 0.0 slice-start.1
  12.5 58.9 %fusion.37 = bf16[1024,3125]{1,0:T(8,128)(2,1)S(1)} fusion(s32[3125]{0:T(1024)S(1)} %get-tuple-element.18, s32[1024]{0:T(1024)S(1)} %xor.202, s32[3125]{0:T(1024)S(1)} %shift-right-logical_xor_fusion.21, f32[64,3125]{1,0:T(8,128)S(1)} %get-tuple-element.14), kind=kLoop, calls=%fused_computation.49 | loop fusion | flops 99200000 | bytes 7229096 | tf_op jit(solution)/shard_map/convert_element_type | solution.py:39
  71.4 0.0 copy-start.5
  71.4 2.7 copy-done.5
  74.1 0.0 slice-done
  74.1 0.0 slice-done.1
  74.1 0.0 copy-start.1
  74.1 8.8 %fusion.67 = f32[1024,1024]{1,0:T(8,128)} fusion(bf16[1024,3125]{1,0:T(8,128)(2,1)S(1)} %fusion.37, bf16[1024,3125]{0,1:T(8,128)(2,1)S(1)} %bitcast.23), kind=kOutput, calls=%fused_computation.103 | convolution fusion | flops 6553600000 | bytes 16994304 | tf_op jit(solution)/shard_map/dot_general | solution.py:88
  83.0 0.0 reduce-scatter.6.cloned.1.call-update
  83.0 0.0 reduce-scatter.8.cloned.1.call-start
  83.0 0.0 copy-done.1
  83.1 0.0 copy-start.2
  83.1 58.9 %fusion.38 = f32[64,16]{1,0:T(8,128)S(1)} fusion(s32[3125]{0:T(1024)S(1)} %get-tuple-element.18, s32[64,16]{1,0:T(8,128)S(1)} %copy.17, s32[3125]{0:T(1024)S(1)} %shift-right-logical_xor_fusion.21), kind=kLoop, calls=%fused_computation.50 | loop fusion | flops 95998976 | bytes 33192 | tf_op jit(solution)/shard_map/reduce_sum | solution.py:41
  142.0 0.1 reshape.111
  142.0 110.4 %all-reduce.2 = (f32[1024]{0:T(1024)S(1)}, f32[64]{0:T(128)S(1)}) all-reduce(f32[1024]{0:T(1024)S(1)} %reshape.111, f32[64]{0:T(128)S(1)} %broadcast_multiply_fusion), channel_id=1, replica_groups=mesh['pts'=8,'coord'=32] {'coord'}, use_global_device_ids=true, to_apply=%region_1.0 | all-reduce | flops 1088 | bytes 8704 | tf_op jit(solution)/shard_map/psum | solution.py:93
  252.4 49.9 %reduce-scatter.6.cloned.1.call-done = f32[32,1024]{1,0:T(8,128)} async-done(((f32[1024,1024]{1,0:T(8,128)}), f32[32,1024]{1,0:T(8,128)}) %reduce-scatter.6.cloned.1.call-update) | async-done | bytes 131088 | tf_op jit(solution)/shard_map/reduce_scatter | solution.py:87
  302.4 0.0 copy-done.2
  302.4 0.9 tanh_convert_fusion
  303.3 0.0 copy-done
  303.3 0.7 fusion.40
  304.0 0.1 fusion.42
  304.2 0.1 reshape.112
  304.3 0.1 reduce_sum.49
  304.4 0.1 dynamic-slice_subtract_fusion
  304.5 0.0 copy-start.3
  304.5 0.1 mul.286
  304.5 0.1 mul.287
  304.6 0.1 broadcast_multiply_fusion.1
  304.7 2.1 convolution_convert_fusion.1
  306.8 0.0 reduce-scatter.8.cloned.1.call-update
  306.9 0.0 all-gather.2.cloned.1.call-start
  306.9 1.1 fusion.66
  308.1 0.0 all-gather.2.cloned.1.call-update
  308.1 0.0 all-reduce.7.cloned.1.call-start
  308.1 221.3 %reduce-scatter.8.cloned.1.call-done = bf16[32,1024]{1,0:T(8,128)(2,1)} async-done(((bf16[1024,1024]{1,0:T(8,128)(2,1)}), bf16[32,1024]{1,0:T(8,128)(2,1)}) %reduce-scatter.8.cloned.1.call-update) | async-done | bytes 65552 | tf_op jit(solution)/shard_map/reduce_scatter | solution.py:110
  529.4 0.0 all-reduce.7.cloned.1.call-update
  529.5 0.0 reduce-scatter.10.cloned.1.call-start
  529.5 108.2 %all-gather.2.cloned.1.call-done = bf16[1024,1024]{1,0:T(8,128)(2,1)} async-done(((bf16[32,1024]{1,0:T(8,128)(2,1)}), bf16[1024,1024]{1,0:T(8,128)(2,1)}) %all-gather.2.cloned.1.call-update) | async-done | bytes 2097168 | tf_op jit(solution)/shard_map/all_gather | solution.py:99
  637.7 12.0 %convolution_convert_fusion = bf16[1024,3125]{0,1:T(8,128)(2,1)} fusion(bf16[1024,1024]{1,0:T(8,128)(2,1)} %all-gather.2.cloned.1.call-done, bf16[1024,3125]{1,0:T(8,128)(2,1)} %copy-done.5), kind=kOutput, calls=%fused_computation.51 | convolution fusion | flops 6556800000 | bytes 14897152 | tf_op jit(solution)/shard_map/dot_general | solution.py:102
  649.7 0.0 copy-done.3
  649.7 0.0 copy-start.4
  649.7 9.2 %copy.19 = bf16[1024,3125]{1,0:T(8,128)(2,1)} copy(bf16[1024,3125]{0,1:T(8,128)(2,1)} %convolution_convert_fusion) | data formatting | bytes 12800000
  658.9 0.0 reduce-scatter.10.cloned.1.call-update
  658.9 0.0 copy-done.4
  658.9 0.6 dynamic-slice
  660.2 0.1 fusion.53
  660.3 96.0 %all-reduce.3 = (bf16[1024]{0:T(1024)(128)(2,1)S(1)}, bf16[1024]{0:T(1024)(128)(2,1)S(1)}) all-reduce(bf16[1024]{0:T(1024)(128)(2,1)S(1)} %get-tuple-element.15, bf16[1024]{0:T(1024)(128)(2,1)S(1)} %multiply_convert_fusion), channel_id=5, replica_groups=mesh['pts'=8,'coord'=32] {'coord'}, use_global_device_ids=true, to_apply=%region_10.0.clone | all-reduce | flops 2048 | bytes 8192
  756.2 0.1 dynamic-slice.1
  756.3 0.1 dynamic-slice.3
  756.4 32.8 %all-reduce.4 = (bf16[32]{0:T(256)(128)(2,1)S(1)}, bf16[32]{0:T(256)(128)(2,1)S(1)}) all-reduce(bf16[32]{0:T(256)(128)(2,1)S(1)} %dynamic-slice.1, bf16[32]{0:T(256)(128)(2,1)S(1)} %dynamic-slice.3), channel_id=1, replica_groups=mesh['pts'=8,'coord'=32] {'pts'}, use_global_device_ids=true, to_apply=%region_11.0 | all-reduce | flops 64 | bytes 256 | tf_op jit(solution)/shard_map/psum | solution.py:122
  789.2 0.5 convert_element_type.86
  789.7 0.5 convert_element_type.88
  790.3 0.0 all-reduce.7.cloned.1.call-done
  790.3 1.5 convert_element_type.85
  791.8 0.0 reduce-scatter.10.cloned.1.call-done
  791.8 2.2 copy.20
  (7 shorter events, 0.1 us)
Async XLA Ops:
  7.2 296.1 %copy-start = (bf16[1024,1024]{1,0:T(8,128)(2,1)S(1)}, bf16[1024,1024]{1,0:T(8,128)(2,1)}, u32[]{:S(2)}) copy-start(bf16[1024,1024]{1,0:T(8,128)(2,1)} %param.12) | copy-start | bytes 6291460
  7.2 295.2 %reduce-scatter.6.cloned.1.call-start = ((), (), s32[]{:S(2)}) async-start(), calls=%async_computation.3 | async-start | bytes 4325376 | tf_op jit(solution)/shard_map/reduce_scatter | solution.py:87
  8.3 65.8 %slice-start = ((s8[6406144]{0:T(1024)(128)(4,1)}), s8[4194304]{0:T(1024)(128)(4,1)S(1)}, s32[]{:S(2)}) async-start(s8[6406144]{0:T(1024)(128)(4,1)} %bitcast.22), calls=%async_computation.8 | async-start | bytes 8388608
  12.4 61.7 %slice-start.1 = ((s8[6406144]{0:T(1024)(128)(4,1)}), s8[2211840]{0:T(1024)(128)(4,1)S(1)}, s32[]{:S(2)}) async-start(s8[6406144]{0:T(1024)(128)(4,1)} %bitcast.22), calls=%async_computation.9 | async-start | bytes 4423680
  71.4 2.7 copy-start.5
  74.1 8.9 %copy-start.1 = (bf16[1024]{0:T(1024)(128)(2,1)S(1)}, bf16[1024]{0:T(1024)(128)(2,1)}, u32[]{:S(2)}) copy-start(bf16[1024]{0:T(1024)(128)(2,1)} %param.13) | copy-start | bytes 6148
  83.0 446.5 %reduce-scatter.8.cloned.1.call-start = ((), (), s32[]{:S(2)}) async-start(), calls=%async_computation.5 | async-start | bytes 2162688 | tf_op jit(solution)/shard_map/reduce_scatter | solution.py:110
  83.1 219.3 %copy-start.2 = (f32[1024]{0:T(1024)S(1)}, f32[1024]{0:T(1024)}, u32[]{:S(2)}) copy-start(f32[1024]{0:T(1024)} %param.11) | copy-start | bytes 12292
  304.5 345.2 %copy-start.3 = (f32[2]{0:T(128)}, f32[2]{0:T(128)S(1)}, u32[]{:S(2)}) copy-start(f32[2]{0:T(128)S(1)} %dynamic-slice_subtract_fusion) | copy-start | bytes 28
  306.9 330.8 %all-gather.2.cloned.1.call-start = ((), (), s32[]{:S(2)}) async-start(), calls=%async_computation.4 | async-start | bytes 2162688 | tf_op jit(solution)/shard_map/all_gather | solution.py:99
  308.1 482.2 %all-reduce.7.cloned.1.call-start = ((), (), s32[]{:S(2)}) async-start(), calls=%async_computation.6 | async-start | bytes 131072 | tf_op jit(solution)/shard_map/psum | solution.py:121
  529.5 262.3 %reduce-scatter.10.cloned.1.call-start = ((), (), s32[]{:S(2)}) async-start(), calls=%async_computation.7 | async-start | bytes 7372800
  649.7 9.2 %copy-start.4 = (u32[256]{0:T(256)S(1)}, u32[256]{0:T(256)}, u32[]{:S(2)}) copy-start(u32[256]{0:T(256)} %constant.76) | copy-start | bytes 3076
Sparse Core Ops, SparseCore 0:
  83.1 219.1 reduce-scatter.5
  307.0 222.4 reduce-scatter.7
  533.5 104.0 all-gather.1
  640.1 66.6 all-reduce.6
  709.2 77.9 reduce-scatter.9
where the time goes:
time: 801 us; the launch traced here: 800 us
  waiting for transfers between devices  379 us (47%)
  blocking collectives  239 us (30%)
  other arithmetic  126 us (16%)
  matrix products  25 us (3%)
  local copies, waits for them, and re-layouts  16.2 us (2%)
  between operations  14.6 us (2%)
    reduce_scatter x1, waiting for transfers between devices, shards(): lax.psum_scatter(grad_second.astype(jnp.bfloat16), 'coord', scatter_dimen...  221 us
    psum x1, blocking collectives, shards(): squares_all, source_all = lax.psum((squares, source), 'coord')  110 us
    all_gather x1, waiting for transfers between devices, shards(): grad_rows = lax.all_gather(grad_pre_one, 'coord', axis=0, tiled=True)  108 us
    unnamed x1, blocking collectives  96 us
    convert_element_type x1, other arithmetic, perturbed_rows(): (coords[:, None, :] + NOISE_SCALE * noise_draw).astype(jnp.bfloat16)  58.9 us
    reduce_sum x1, other arithmetic, perturbed_rows(): jnp.sum(noise_draw * noise_draw, axis=2)  58.9 us
    reduce_scatter x1, waiting for transfers between devices, shards(): lax.psum_scatter(lax.dot_general(picked, w1, (((1,), (1,)), ((), ())), pr...  49.9 us
    psum x1, blocking collectives, shards(): lax.psum(share_bias.astype(jnp.bfloat16), 'pts').astype(jnp.float32)  32.8 us
  transfers between devices with their start and end apart: 5, of which 3 were waited for; matrix products, arithmetic and copies ran while one was open for 11% of the time, Pallas kernels for 0%

commit v1 on v0

--- a/solution.py
+++ b/solution.py
@@ -3,11 +3,19 @@
 import jax.numpy as jnp
 from jax import lax
 from jax.sharding import PartitionSpec as P
+from jax.lax import all_to_all, psum
 
 D = 100000
 hash_factor = 73244475
 NOISE_SCALE = 2.0
 READOUT = 0.0625
+
+
+def begin_rows(block_here, out_dim):
+    field_out = jnp.concatenate(
+        all_to_all(jnp.stack(psum(1, "coord") * [block_here], axis=0), "coord", 0, 0), out_dim
+    )
+    return field_out
 
 
 def shuffle_bits(packed_bits):
@@ -96,7 +104,7 @@
     residual, grad_pre_one, grad_second, grad_bias, grad_readout, hidden_one, grad_pre_two = (
         hidden_pass(pre_local + b1[None, :], squares_local, source_local, w2, w3, samples)
     )
-    grad_rows = lax.all_gather(grad_pre_one, "coord", axis=0, tiled=True)
+    grad_rows = begin_rows(grad_pre_one, 0)
     picked = grad_rows
     grad_first = lax.psum_scatter(
         lax.dot_general(

time: 801 us -> 733 us (0.915)
  waiting for transfers between devices: 379 us -> 284 us
  blocking collectives: 239 us -> 260 us
    all_gather x1 -> x0, waiting for transfers between devices: 108 us -> none  [shards(): grad_rows = lax.all_gather(grad_pre_one, 'coord', axis=0, tiled=True)]
    convert_element_type x1 -> x2, other arithmetic: 58.9 us -> 121 us  [perturbed_rows(): (coords[:, None, :] + NOISE_SCALE * noise_draw).astype(jnp.bfloat16)]
    reduce_sum x1 -> x0, other arithmetic: 58.9 us -> none  [perturbed_rows(): jnp.sum(noise_draw * noise_draw, axis=2)]
    psum x1, blocking collectives: 32.8 us -> 53.5 us  [shards(): lax.psum(share_bias.astype(jnp.bfloat16), 'pts').astype(jnp.float32)]
    reduce_scatter x1, waiting for transfers between devices: 221 us -> 236 us  [shards(): lax.psum_scatter(grad_second.astype(jnp.bfloat16), 'coord', scatter_dimen...]
  transfers between devices with their start and end apart: 5 -> 5, of which waited for: 3 -> 2; matrix products, arithmetic and copies ran while one was open for 11% -> 12% of each run, Pallas kernels for 0% -> 0%
where the time goes in v1:
time: 733 us; the launch traced here: 732 us
  waiting for transfers between devices  284 us (39%)
  blocking collectives  260 us (35%)
  other arithmetic  129 us (18%)
  matrix products  24.5 us (3%)
  local copies, waits for them, and re-layouts  15 us (2%)
  between operations  14.6 us (2%)
    reduce_scatter x1, waiting for transfers between devices, shards(): lax.psum_scatter(grad_second.astype(jnp.bfloat16), 'coord', scatter_dimen...  236 us
    convert_element_type x2, other arithmetic, perturbed_rows(): (coords[:, None, :] + NOISE_SCALE * noise_draw).astype(jnp.bfloat16)  121 us
    psum x1, blocking collectives, shards(): squares_all, source_all = lax.psum((squares, source), 'coord')  110 us
    unnamed x1, blocking collectives  96.8 us
    psum x1, blocking collectives, shards(): lax.psum(share_bias.astype(jnp.bfloat16), 'pts').astype(jnp.float32)  53.5 us
    reduce_scatter x1, waiting for transfers between devices, shards(): lax.psum_scatter(lax.dot_general(picked, w1, (((1,), (1,)), ((), ())), pr...  47.8 us
  transfers between devices with their start and end apart: 5, of which 2 were waited for; matrix products, arithmetic and copies ran while one was open for 12% of the time, Pallas kernels for 0%

profile of v1, /device:TPU:1, one launch (start us, length us, event | category | flops | bytes accessed | tf_op | source)
XLA Modules:
  0.0 732.0 jit_solution(5503498493576188559)
XLA Ops:
  7.2 0.0 copy-start
  7.2 0.0 reduce-scatter.6.cloned.1.call-start
  7.3 0.9 copy.17
  8.2 0.1 xor.258
  8.3 0.0 slice-start
  8.3 4.2 multiply_reduce_fusion.1
  12.4 0.0 slice-start.1
  12.5 58.9 %fusion.36 = bf16[1024,3125]{1,0:T(8,128)(2,1)S(1)} fusion(s32[3125]{0:T(1024)S(1)} %get-tuple-element.20, s32[1024]{0:T(1024)S(1)} %xor.258, s32[3125]{0:T(1024)S(1)} %shift-right-logical_xor_fusion.21, f32[64,3125]{1,0:T(8,128)S(1)} %get-tuple-element.16), kind=kLoop, calls=%fused_computation.49 | loop fusion | flops 99200000 | bytes 7229096 | tf_op jit(solution)/shard_map/convert_element_type | solution.py:47
  71.4 0.0 slice-done
  71.4 0.0 slice-done.1
  71.4 0.0 copy-start.1
  71.4 8.8 %fusion.65 = f32[1024,1024]{1,0:T(8,128)} fusion(bf16[1024,3125]{1,0:T(8,128)(2,1)S(1)} %fusion.36, bf16[1024,3125]{0,1:T(8,128)(2,1)S(1)} %bitcast.25), kind=kOutput, calls=%fused_computation.103 | convolution fusion | flops 6553600000 | bytes 16994304 | tf_op jit(solution)/shard_map/dot_general | solution.py:96
  80.3 0.0 reduce-scatter.6.cloned.1.call-update
  80.3 0.0 reduce-scatter.8.cloned.1.call-start
  80.3 0.0 copy-done.1
  80.4 0.0 copy-start.2
  80.4 61.9 %add_convert_fusion = (bf16[64,16,3125]{2,1,0:T(8,128)(2,1)}, f32[64,16]{1,0:T(8,128)S(1)}) fusion(f32[64,3125]{1,0:T(8,128)S(1)} %get-tuple-element.16, s32[3125]{0:T(1024)S(1)} %get-tuple-element.20, s32[64,16]{1,0:T(8,128)S(1)} %copy.17, s32[3125]{0:T(1024)S(1)} %shift-right-logical_xor_fusion.21), kind=kLoop, calls=%fused_computation.48 | loop fusion | flops 105598976 | bytes 7233192 | tf_op jit(solution)/shard_map/convert_element_type | solution.py:47
  142.2 0.1 reshape.203
  142.3 110.0 %all-reduce.2 = (f32[1024]{0:T(1024)S(1)}, f32[64]{0:T(128)S(1)}) all-reduce(f32[1024]{0:T(1024)S(1)} %reshape.203, f32[64]{0:T(128)S(1)} %broadcast_multiply_fusion), channel_id=1, replica_groups=mesh['pts'=8,'coord'=32] {'coord'}, use_global_device_ids=true, to_apply=%region_1.0 | all-reduce | flops 1088 | bytes 8704 | tf_op jit(solution)/shard_map/psum | solution.py:101
  252.3 47.8 %reduce-scatter.6.cloned.1.call-done = f32[32,1024]{1,0:T(8,128)} async-done(((f32[1024,1024]{1,0:T(8,128)}), f32[32,1024]{1,0:T(8,128)}) %reduce-scatter.6.cloned.1.call-update) | async-done | bytes 131088 | tf_op jit(solution)/shard_map/reduce_scatter | solution.py:95
  300.1 0.0 copy-done.2
  300.1 0.9 tanh_convert_fusion
  301.0 0.0 copy-done
  301.0 0.7 fusion.38
  301.8 0.1 fusion.40
  301.9 0.1 reshape.204
  302.0 0.1 reduce_sum.49
  302.1 0.1 dynamic-slice_subtract_fusion
  302.2 0.0 copy-start.3
  302.2 0.1 mul.353
  302.3 0.1 mul.354
  302.3 0.1 broadcast_multiply_fusion.1
  302.4 2.2 convolution_convert_fusion.1
  304.6 0.0 reduce-scatter.8.cloned.1.call-update
  304.6 0.5 fusion.64
  305.2 1.6 stack.2
  306.8 4.8 all-to-all-start
  311.5 0.0 all-reduce.7.cloned.1.call-start
  311.6 236.0 %reduce-scatter.8.cloned.1.call-done = bf16[32,1024]{1,0:T(8,128)(2,1)} async-done(((bf16[1024,1024]{1,0:T(8,128)(2,1)}), bf16[32,1024]{1,0:T(8,128)(2,1)}) %reduce-scatter.8.cloned.1.call-update) | async-done | bytes 65552 | tf_op jit(solution)/shard_map/reduce_scatter | solution.py:118
  547.6 0.0 all-reduce.7.cloned.1.call-update
  547.7 0.0 reduce-scatter.10.cloned.1.call-start
  547.7 0.0 all-to-all-done
  547.7 12.0 %convolution_convert_fusion = bf16[1024,3125]{0,1:T(8,128)(2,1)} fusion(bf16[1024,1024]{1,0:T(8,128)(2,1)} %bitcast.2, bf16[1024,3125]{1,0:T(8,128)(2,1)} %bitcast.26), kind=kOutput, calls=%fused_computation.51 | convolution fusion | flops 6556800000 | bytes 14897152 | tf_op jit(solution)/shard_map/dot_general | solution.py:110
  559.8 0.0 copy-done.3
  559.8 0.0 copy-start.4
  559.8 9.2 %copy.19 = bf16[1024,3125]{1,0:T(8,128)(2,1)} copy(bf16[1024,3125]{0,1:T(8,128)(2,1)} %convolution_convert_fusion) | data formatting | bytes 12800000
  568.9 0.0 reduce-scatter.10.cloned.1.call-update
  569.0 0.0 copy-done.4
  569.0 0.6 dynamic-slice
  570.2 0.1 fusion.51
  570.3 96.8 %all-reduce.3 = (bf16[1024]{0:T(1024)(128)(2,1)S(1)}, bf16[1024]{0:T(1024)(128)(2,1)S(1)}) all-reduce(bf16[1024]{0:T(1024)(128)(2,1)S(1)} %get-tuple-element.17, bf16[1024]{0:T(1024)(128)(2,1)S(1)} %multiply_convert_fusion), channel_id=5, replica_groups=mesh['pts'=8,'coord'=32] {'coord'}, use_global_device_ids=true, to_apply=%region_10.0.clone | all-reduce | flops 2048 | bytes 8192
  667.1 0.1 dynamic-slice.1
  667.2 0.1 dynamic-slice.3
  667.3 53.5 %all-reduce.4 = (bf16[32]{0:T(256)(128)(2,1)S(1)}, bf16[32]{0:T(256)(128)(2,1)S(1)}) all-reduce(bf16[32]{0:T(256)(128)(2,1)S(1)} %dynamic-slice.1, bf16[32]{0:T(256)(128)(2,1)S(1)} %dynamic-slice.3), channel_id=1, replica_groups=mesh['pts'=8,'coord'=32] {'pts'}, use_global_device_ids=true, to_apply=%region_11.0 | all-reduce | flops 64 | bytes 256 | tf_op jit(solution)/shard_map/psum | solution.py:130
  720.8 0.5 convert_element_type.113
  721.3 0.5 convert_element_type.115
  721.8 0.0 all-reduce.7.cloned.1.call-done
  721.8 1.5 convert_element_type.112
  723.3 0.0 reduce-scatter.10.cloned.1.call-done
  723.3 2.2 copy.20
  (7 shorter events, 0.1 us)
Async XLA Ops:
  7.2 293.9 %copy-start = (bf16[1024,1024]{1,0:T(8,128)(2,1)S(1)}, bf16[1024,1024]{1,0:T(8,128)(2,1)}, u32[]{:S(2)}) copy-start(bf16[1024,1024]{1,0:T(8,128)(2,1)} %param.12) | copy-start | bytes 6291460
  7.2 292.9 %reduce-scatter.6.cloned.1.call-start = ((), (), s32[]{:S(2)}) async-start(), calls=%async_computation.4 | async-start | bytes 4325376 | tf_op jit(solution)/shard_map/reduce_scatter | solution.py:95
  8.3 63.1 %slice-start = ((s8[6406144]{0:T(1024)(128)(4,1)}), s8[4194304]{0:T(1024)(128)(4,1)S(1)}, s32[]{:S(2)}) async-start(s8[6406144]{0:T(1024)(128)(4,1)} %bitcast.24), calls=%async_computation.8 | async-start | bytes 8388608
  12.4 59.0 %slice-start.1 = ((s8[6406144]{0:T(1024)(128)(4,1)}), s8[2211840]{0:T(1024)(128)(4,1)S(1)}, s32[]{:S(2)}) async-start(s8[6406144]{0:T(1024)(128)(4,1)} %bitcast.24), calls=%async_computation.9 | async-start | bytes 4423680
  71.4 8.9 %copy-start.1 = (bf16[1024]{0:T(1024)(128)(2,1)S(1)}, bf16[1024]{0:T(1024)(128)(2,1)}, u32[]{:S(2)}) copy-start(bf16[1024]{0:T(1024)(128)(2,1)} %param.13) | copy-start | bytes 6148
  80.3 467.4 %reduce-scatter.8.cloned.1.call-start = ((), (), s32[]{:S(2)}) async-start(), calls=%async_computation.5 | async-start | bytes 2162688 | tf_op jit(solution)/shard_map/reduce_scatter | solution.py:118
  80.4 219.7 %copy-start.2 = (f32[1024]{0:T(1024)S(1)}, f32[1024]{0:T(1024)}, u32[]{:S(2)}) copy-start(f32[1024]{0:T(1024)} %param.11) | copy-start | bytes 12292
  302.2 257.6 %copy-start.3 = (f32[2]{0:T(128)}, f32[2]{0:T(128)S(1)}, u32[]{:S(2)}) copy-start(f32[2]{0:T(128)S(1)} %dynamic-slice_subtract_fusion) | copy-start | bytes 28
  306.8 241.0 %all-to-all-start = ((bf16[32,32,1024]{2,1,0:T(8,128)(2,1)}), bf16[32,32,1024]{2,1,0:T(8,128)(2,1)}, u32[]{:S(2)}, u32[]{:S(2)}) async-start(bf16[32,32,1024]{2,1,0:T(8,128)(2,1)} %stack.2), calls=%async_computation.1 | async-start | bytes 4194304 | tf_op jit(solution)/shard_map/all_to_all | solution.py:16
  311.5 410.3 %all-reduce.7.cloned.1.call-start = ((), (), s32[]{:S(2)}) async-start(), calls=%async_computation.6 | async-start | bytes 131072 | tf_op jit(solution)/shard_map/psum | solution.py:129
  547.7 175.6 %reduce-scatter.10.cloned.1.call-start = ((), (), s32[]{:S(2)}) async-start(), calls=%async_computation.7 | async-start | bytes 7372800
  559.8 9.2 %copy-start.4 = (u32[256]{0:T(256)S(1)}, u32[256]{0:T(256)}, u32[]{:S(2)}) copy-start(u32[256]{0:T(256)} %constant.76) | copy-start | bytes 3076
Sparse Core Ops, SparseCore 0:
  80.4 219.6 reduce-scatter.5
  304.8 242.8 reduce-scatter.7
  550.3 86.4 all-reduce.6
  639.2 77.7 reduce-scatter.9
